TPU v7x, 32 devices: a whole 2x2x4 slice. The times are simulated.
32 devices in a mesh: tm: 16 (over z, y, core), rows: 2 (over x).
Axes of the slice: x: 2, y: 2, z: 4, core: 2. Of those that a mesh axis runs over, the one named last changes fastest.
Arguments:
- latents: bfloat16 [128, 4, 32, 512], P('tm', 'rows'), may hold values from -6 to 6
- clip_ids: int32 [128], replicated, may hold values from 0 to 24, never falling along the last dimension, each value on 1 to 9 neighbouring positions
- gain_in: float32 [512], replicated, may hold values from 0.25 to 1.75
- w_space: bfloat16 [3, 3, 512, 512], P(None, None, None, 'tm'), may hold values from -0.09375 to 0.09375
- w_time: bfloat16 [3, 512, 512], replicated, may hold values from -0.15625 to 0.15625
- gain_attn: float32 [512], replicated, may hold values from 0.25 to 1.75
- w_qkv: bfloat16 [512, 1536], replicated, may hold values from -0.25 to 0.25
- w_out: bfloat16 [512, 512], replicated, may hold values from -0.25 to 0.25
Outputs:
- block_out: bfloat16 [128, 4, 32, 512], P('tm', 'rows')
Inputs may be any that keep to these rules, and one draw needn't show every extreme that they name: `clip_ids`: clip numbers never fall along time; each clip has 1 to 9 frames and some clip has exactly 9.
All inputs are finite; a program needn't handle non-finite values.
Results may differ from a plain program's by a relative error of at most 0.0085.
Values may be sent and summed in bfloat16 or wider, within the bound.
No kernel may reach another device: no remote copies, remote signals or barrier semaphores. Data moves between devices by JAX's collectives and lax.ppermute only.
A program may use at most 64 MiB of HBM per device.

v0:
```python
import jax
import jax.numpy as jnp
from jax import lax
from jax.sharding import PartitionSpec as P


def with_halo(cells, sides, width):
    for axis, dim in sides:
        count = lax.axis_size(axis)
        ends = count - 1
        head = lax.slice_in_dim(cells, 0, width, axis=dim)
        tail = lax.slice_in_dim(cells, cells.shape[dim] - width, cells.shape[dim], axis=dim)
        cells = jnp.concatenate(
            [
                lax.ppermute(tail, axis, [(i, (i + 1) % count) for i in range(ends)]),
                cells,
                lax.ppermute(head, axis, [((i + 1) % count, i) for i in range(ends)]),
            ],
            axis=dim,
        )
    return cells


def shifted(array, axis, by):
    length = lax.axis_size(axis)
    pairs = [(i, i + by) for i in range(length) if 0 <= i + by < length]
    return lax.ppermute(array, axis, pairs)


def entering(array, axis, combine, identity):
    length, index = (lax.axis_size(axis), lax.axis_index(axis))
    everything = jax.tree.map(
        lambda part, kind: lax.all_gather(part.astype(kind), axis),
        array,
        (jnp.bfloat16, jnp.bfloat16, jnp.bfloat16),
    )
    start = jax.tree.map(
        lambda part, zero: jnp.broadcast_to(jnp.asarray(zero, part.dtype), part.shape),
        array,
        identity,
    )

    def step(k, before):
        reached = k < index
        new = combine(
            before, jax.tree.map(lambda part, own: part[k].astype(own.dtype), everything, array)
        )
        return jax.tree.map(lambda a, b: jnp.where(reached, a, b), new, before)

    return lax.fori_loop(0, length, step, start)


def rms_scale(values, gain):
    floats = values.astype(jnp.float32)
    scale = lax.rsqrt(jnp.mean(floats * floats, axis=-1, keepdims=True) + 1e-06)
    return (floats * scale * gain).astype(jnp.bfloat16)


def join_clip(earlier, later):
    early_sum, early_num, early_flag = earlier
    late_sum, late_num, late_flag = later
    pick = late_flag > 0
    return (
        jnp.where(pick, late_sum, early_sum + late_sum),
        jnp.where(pick, late_num, early_num + late_num),
        jnp.maximum(early_flag, late_flag),
    )


def attend_frames(tokens, chans):
    query = tokens[:, :, :chans]
    key = tokens[:, :, chans : 2 * chans]
    value = tokens[:, :, 2 * chans :]
    scores = jnp.einsum("fqc,fkc->fqk", query, key, preferred_element_type=jnp.float32) * chans ** (
        -0.5
    )
    probs = jax.nn.softmax(scores, axis=-1).astype(jnp.bfloat16)
    return jnp.einsum("fqk,fkc->fqc", probs, value, preferred_element_type=jnp.float32).astype(
        jnp.bfloat16
    )


def local(latents, clip_ids, gain_in, w_space, w_time, gain_attn, w_qkv, w_out):
    frames, height, width, chans = latents.shape
    groups = lax.axis_size("rows")
    normed = rms_scale(latents, gain_in)
    padded = with_halo(normed, (("rows", 1),), 1)
    padded = jnp.pad(padded, ((0, 0), (0, 0), (1, 1), (0, 0)))
    windows = [
        padded[:, dy : dy + height, dx : dx + width, :].reshape(-1, chans)
        for dy in range(3)
        for dx in range(3)
    ]
    piece = lax.all_gather(w_space, "tm", axis=3, tiled=True)
    total = jnp.zeros((windows[0].shape[0], piece.shape[3]), jnp.float32)
    for dy in range(3):
        for dx in range(3):
            total = total + jnp.dot(
                windows[dy * 3 + dx], piece[dy, dx], preferred_element_type=jnp.float32
            )
    conv = total
    acts = jax.nn.silu(conv).astype(jnp.bfloat16).reshape(frames, height, width, chans)
    earlier = shifted(acts[frames - 2 :], "tm", 1)
    extended = jnp.concatenate([earlier, acts], 0)
    first = lax.axis_index("tm") * frames
    seg_pad = jnp.concatenate([jnp.full((2,), -1, jnp.int32), clip_ids])
    seg_ext = lax.dynamic_slice_in_dim(seg_pad, first, frames + 2)
    segs = seg_ext[2:]
    total = latents.astype(jnp.float32).reshape(-1, chans)
    for back in range(3):
        source = extended[2 - back : 2 - back + frames]
        keep = (seg_ext[2 - back : 2 - back + frames] == segs).astype(jnp.bfloat16)[
            :, None, None, None
        ]
        total = total + jnp.dot(
            (source * keep).reshape(-1, chans), w_time[back], preferred_element_type=jnp.float32
        )
    resid = total.astype(jnp.bfloat16).reshape(frames, height, width, chans)
    floats = resid.astype(jnp.float32)
    sums_local = []
    nums_local = []
    running = floats[0]
    number = jnp.float32(1.0)
    sums_local.append(running)
    nums_local.append(number)
    for index in range(1, frames):
        same = segs[index] == segs[index - 1]
        running = jnp.where(same, running, jnp.float32(0.0)) + floats[index]
        number = jnp.where(same, number, jnp.float32(0.0)) + jnp.float32(1.0)
        sums_local.append(running)
        nums_local.append(number)
    last_num = jnp.reshape(number, (1,))
    flag = jnp.reshape((segs[frames - 1] != seg_ext[1]).astype(jnp.float32), (1,))
    empty = (jnp.zeros_like(running), jnp.zeros((1,), jnp.float32), jnp.zeros((1,), jnp.float32))
    carry_sum, carry_num, carry_flag = entering((running, last_num, flag), "tm", join_clip, empty)
    mixed_list = []
    for index in range(frames):
        cont = segs[index] == seg_ext[1]
        clip_sum = sums_local[index] + jnp.where(cont, carry_sum, jnp.float32(0.0))
        clip_num = nums_local[index] + jnp.where(cont, carry_num[0], jnp.float32(0.0))
        mixed_list.append((floats[index] + clip_sum / clip_num).astype(jnp.bfloat16))
    mixed = jnp.stack(mixed_list, 0)
    attn_in = rms_scale(mixed, gain_attn)
    qkv = jnp.dot(attn_in.reshape(-1, chans), w_qkv, preferred_element_type=jnp.float32).astype(
        jnp.bfloat16
    )
    grouped = qkv.reshape(groups, frames // groups, height, width, 3 * chans)
    block = lax.all_to_all(grouped, "rows", split_axis=0, concat_axis=2, tiled=True)
    count = block.shape[1]
    tokens = block.reshape(count, -1, 3 * chans)
    out = attend_frames(tokens, chans)
    attended = out.reshape(1, count, height * groups, width, chans)
    returned = lax.all_to_all(attended, "rows", split_axis=2, concat_axis=0, tiled=True)
    result = mixed.astype(jnp.float32).reshape(-1, chans) + jnp.dot(
        returned.reshape(-1, chans), w_out, preferred_element_type=jnp.float32
    )
    return result.astype(jnp.bfloat16).reshape(frames, height, width, chans)


def solution(mesh):
    placed = (P("tm", "rows", None, None), P(), P(), P(None, None, None, "tm"), P(), P(), P(), P())
    return jax.shard_map(
        local, mesh=mesh, in_specs=placed, out_specs=P("tm", "rows", None, None), check_vma=False
    )
```

profile of v0, /device:TPU:0, one launch (start us, length us, event | category | flops | bytes accessed | tf_op | source)
XLA Modules:
  0.0 244.3 jit_solution(15914931476498741329)
XLA Ops:
  8.6 1.2 multiply_convert_fusion.1
  9.9 4.9 %collective-permute-start = (bf16[8,1,32,512]{3,2,1,0:T(8,128)(2,1)S(1)}, bf16[8,1,32,512]{3,2,1,0:T(8,128)(2,1)S(1)}, u32[]{:S(2)}, u32[]{:S(2)}) collective-permute-start(bf16[8,1,32,512]{3,2,1,0:T(8,128)(2,1)S(1)} %get-tuple-element.195), channel_id=1, source_target_pairs={{0,1},{2,3},{4,5},{6,7},{8,9},{10,11},{12,13},{14,15},{16,17},{18,... | collective-permute-start | bytes 786440 | tf_op jit(solution)/shard_map/ppermute | solution.py:15
  14.7 1.3 collective-permute-start.1
  27.5 1.7 fusion.34
  29.2 36.5 %all-gather.4.cloned.1.call-done = bf16[3,3,512,512]{2,3,1,0:T(8,128)(2,1)} async-done(((bf16[3,3,512,32]{2,3,1,0:T(8,128)(2,1)}), bf16[3,3,512,512]{2,3,1,0:T(8,128)(2,1)}) %all-gather.4.cloned.1.call-update) | async-done | bytes 4718608 | tf_op jit(solution)/shard_map/all_gather | solution.py:94
  65.7 1.8 fusion.23
  67.5 1.7 fusion.22
  69.2 1.6 convolution_add_fusion.10
  74.9 2.2 collective-permute-start.2
  81.8 1.4 dynamic-update-slice
  83.2 31.5 %all-reduce.4 = (bf16[16]{0:T(256)(128)(2,1)S(1)}, bf16[16]{0:T(256)(128)(2,1)S(1)}) all-reduce(bf16[16]{0:T(256)(128)(2,1)S(1)} %dynamic-update-slice, bf16[16]{0:T(256)(128)(2,1)S(1)} %dynamic-update-slice.1), channel_id=2, replica_groups=mesh['tm'=16,'rows'=2] {'tm'}, use_global_device_ids=true, to_apply=%add.2 | all-reduce | flops 32 | bytes 128
  125.0 75.8 %while.16 = (s32[]{:T(128)}, f32[2,32,512]{2,1,0:T(8,128)S(1)}, f32[1]{0:T(128)}, s32[]{:T(128)}, bf16[16,1]{0,1:T(2,128)(2,1)S(1)}, /*index=5*/bf16[16,2,32,512...) while((s32[]{:T(128)}, f32[2,32,512]{2,1,0:T(8,128)S(1)}, f32[1]{0:T(128)}, ...), condition=%wide.region_2.3_spmd.clone, body=%wide.region_1.2_spmd.clone.sunk | while | flops 163849 | bytes 327847 | solution.py:50
  128.2 1.5 fusion.61
  133.0 1.5 fusion.61
  137.7 1.5 fusion.61
  142.4 1.5 fusion.61
  147.2 1.5 fusion.61
  151.9 1.5 fusion.61
  156.6 1.5 fusion.61
  161.4 1.5 fusion.61
  166.1 1.5 fusion.61
  170.9 1.5 fusion.61
  175.6 1.5 fusion.61
  180.3 1.5 fusion.61
  185.1 1.5 fusion.61
  189.8 1.5 fusion.61
  194.6 1.5 fusion.61
  199.3 1.5 fusion.61
  203.0 20.9 %all_to_all.30 = bf16[2,4,2,32,1536]{4,3,2,1,0:T(8,128)(2,1)S(1)} all-to-all(bf16[2,4,2,32,1536]{4,3,2,1,0:T(8,128)(2,1)S(1)} %bitcast.174), channel_id=1, replica_groups=mesh['tm'=16,'rows'=2] {'rows'}, dimensions={0} | all-to-all | bytes 3145728 | tf_op jit(solution)/shard_map/all_to_all | solution.py:148
  225.6 1.4 convolution_convert_fusion.1
  227.1 9.1 %all_to_all.31 = bf16[1,4,4,32,512]{4,3,1,0,2:T(8,128)(2,1)S(1)} all-to-all(bf16[1,4,4,32,512]{4,3,1,0,2:T(8,128)(2,1)S(1)} %copy.18), channel_id=1, replica_groups=mesh['tm'=16,'rows'=2] {'rows'}, dimensions={2} | all-to-all | bytes 1048576 | tf_op jit(solution)/shard_map/all_to_all | solution.py:153
  236.3 1.2 fusion.11
  (118 shorter events, 38.2 us)
Async XLA Ops:
  6.5 195.4 %copy-start = (bf16[512,1536]{1,0:T(8,128)(2,1)S(1)}, bf16[512,1536]{1,0:T(8,128)(2,1)}, u32[]{:S(2)}) copy-start(bf16[512,1536]{1,0:T(8,128)(2,1)} %param.16) | copy-start | bytes 4718596
  6.5 9.5 %copy-start.14 = (s32[128]{0:T(128)S(1)}, s32[128]{0:T(128)}, u32[]{:S(2)}) copy-start(s32[128]{0:T(128)} %param.11) | copy-start | bytes 1540
  6.5 59.2 %all-gather.4.cloned.1.call-start = ((), (), s32[]{:S(2)}) async-start(), calls=%async_computation.2 | async-start | bytes 5013504 | tf_op jit(solution)/shard_map/all_gather | solution.py:94
  7.3 117.8 %all-gather.6.cloned.1.call-start = ((), (), s32[]{:S(2)}) async-start(), calls=%async_computation.3 | async-start | bytes 1114112 | tf_op jit(solution)/shard_map/all_gather | solution.py:33
  9.9 15.8 %collective-permute-start = (bf16[8,1,32,512]{3,2,1,0:T(8,128)(2,1)S(1)}, bf16[8,1,32,512]{3,2,1,0:T(8,128)(2,1)S(1)}, u32[]{:S(2)}, u32[]{:S(2)}) collective-permute-start(bf16[8,1,32,512]{3,2,1,0:T(8,128)(2,1)S(1)} %get-tuple-element.195), channel_id=1, source_target_pairs={{0,1},{2,3},{4,5},{6,7},{8,9},{10,11},{12,13},{14,15},{16,17},{18,... | collective-permute-start | bytes 786440 | tf_op jit(solution)/shard_map/ppermute | solution.py:15
  14.7 11.0 %collective-permute-start.1 = (bf16[8,1,32,512]{3,2,1,0:T(8,128)(2,1)S(1)}, bf16[8,1,32,512]{3,2,1,0:T(8,128)(2,1)S(1)}, u32[]{:S(2)}, u32[]{:S(2)}) collective-permute-start(bf16[8,1,32,512]{3,2,1,0:T(8,128)(2,1)S(1)} %get-tuple-element.196), channel_id=1, source_target_pairs={{1,0},{3,2},{5,4},{7,6},{9,8},{11,10},{13,12},{15,14},{17,16},{19,... | collective-permute-start | bytes 786440 | tf_op jit(solution)/shard_map/ppermute | solution.py:17
  65.7 1.8 copy-start.5
  65.7 3.4 %copy-start.6 = (bf16[8,2,32,512]{3,2,1,0:T(8,128)(2,1)S(1)}, bf16[8,2,32,512]{3,2,1,0:T(8,128)(2,1)}, u32[]{:S(2)}) copy-start(bf16[8,2,32,512]{3,2,1,0:T(8,128)(2,1)} %get-tuple-element.194) | copy-start | bytes 1572868
  67.5 3.3 %copy-start.2 = (bf16[3,3,512,512]{2,3,1,0:T(8,128)(2,1)S(1)}, bf16[3,3,512,512]{2,3,1,0:T(8,128)(2,1)}, u32[]{:S(2)}) copy-start(bf16[3,3,512,512]{2,3,1,0:T(8,128)(2,1)} %all-gather.4.cloned.1.call-done) | copy-start | bytes 14155780
  69.1 1.6 copy-start.4
  70.7 1.0 copy-start.3
  73.2 1.0 copy-start.10
  74.3 2.8 %copy-start.1 = (bf16[8,2,32,512]{3,2,1,0:T(8,128)(2,1)S(1)}, bf16[8,2,32,512]{3,2,1,0:T(8,128)(2,1)}, u32[]{:S(2)}) copy-start(bf16[8,2,32,512]{3,2,1,0:T(8,128)(2,1)} %param.10) | copy-start | bytes 1572868
  74.3 2.8 %copy-start.8 = (bf16[3,512,512]{2,1,0:T(8,128)(2,1)S(1)}, bf16[3,512,512]{2,1,0:T(8,128)(2,1)}, u32[]{:S(2)}) copy-start(bf16[3,512,512]{2,1,0:T(8,128)(2,1)} %param.14) | copy-start | bytes 4718596
  74.9 3.1 %collective-permute-start.2 = (bf16[2,2,32,512]{3,2,1,0:T(8,128)(2,1)S(1)}, bf16[2,2,32,512]{3,2,1,0:T(8,128)(2,1)S(1)}, u32[]{:S(2)}, u32[]{:S(2)}) collective-permute-start(bf16[2,2,32,512]{3,2,1,0:T(8,128)(2,1)S(1)} %bitcast.187), channel_id=1, source_target_pairs={{0,2},{2,4},{4,6},{6,8},{8,10},{10,12},{12,14},{14,16},{16,18},{18... | collective-permute-start | bytes 393224 | tf_op jit(solution)/shard_map/ppermute | solution.py:27
  79.1 1.4 copy-start.15
  125.0 76.0 %copy-start.12 = (f32[64,512]{1,0:T(8,128)S(1)}, f32[64,512]{1,0:T(8,128)}, u32[]{:S(2)}) copy-start(f32[64,512]{1,0:T(8,128)} %get-tuple-element.188) | copy-start | bytes 393220
  125.0 76.1 %copy-start.11 = (f32[64,512]{1,0:T(8,128)S(1)}, f32[64,512]{1,0:T(8,128)}, u32[]{:S(2)}) copy-start(f32[64,512]{1,0:T(8,128)} %get-tuple-element.186) | copy-start | bytes 393220
  201.1 0.7 copy-start.13
  224.0 1.2 copy-start.7
  227.0 9.2 %copy-start.9 = (bf16[512,512]{1,0:T(8,128)(2,1)S(1)}, bf16[512,512]{1,0:T(8,128)(2,1)}, u32[]{:S(2)}) copy-start(bf16[512,512]{1,0:T(8,128)(2,1)} %param.17) | copy-start | bytes 1572868
Sparse Core Ops, SparseCore 0:
  9.5 56.0 all-gather.3
  80.0 40.4 all-gather.5
where the time goes:
time: 246 us; the launch traced here: 244 us
  blocking collectives  61.5 us (25%)
  other arithmetic  41.5 us (17%)
  waiting for transfers between devices  37.7 us (15%)
  between operations  32.4 us (13%)
  loops' own time  31.1 us (13%)
  local copies, waits for them, and re-layouts  18.6 us (8%)
  matrix products  13.2 us (5%)
  starting transfers between devices  8.35 us (3%)
    all_gather x1, waiting for transfers between devices, local(): piece = lax.all_gather(w_space, 'tm', axis=3, tiled=True)  36.5 us
    unnamed x1, blocking collectives  31.5 us
    another operation x1, loops' own time, entering(): return lax.fori_loop(0, length, step, start)  31.1 us
    select_n x16, other arithmetic, step(): return jax.tree.map(lambda a, b: jnp.where(reached, a, b), new, before)  24.5 us
    all_to_all x1, blocking collectives, local(): lax.all_to_all(grouped, 'rows', split_axis=0, concat_axis=2, tiled=True)  20.9 us
    gt x16, other arithmetic, join_clip(): pick = late_flag > 0  10.4 us
    dynamic_slice x16, local copies, waits for them, and re-layouts, step(): part[k].astype(own.dtype)  9.82 us
    all_to_all x1, blocking collectives, local(): lax.all_to_all(attended, 'rows', split_axis=2, concat_axis=0, tiled=True)  9.12 us
  transfers between devices with their start and end apart: 5, of which 2 were waited for; matrix products, arithmetic and copies ran while one was open for 5% of the time, Pallas kernels for 0%

commit v1 on v0

--- a/solution.py
+++ b/solution.py
@@ -2,6 +2,34 @@
 import jax.numpy as jnp
 from jax import lax
 from jax.sharding import PartitionSpec as P
+from jax.lax import axis_index, axis_size, ppermute
+
+
+def touch_types(frame):
+    axis_name = "tm"
+    arr_out, mat_out, val = (axis_size(axis_name), axis_index(axis_name), frame.shape[3])
+    now = lax.dynamic_update_slice_in_dim(
+        jnp.zeros(
+            [num * arr_out if dd == 3 else num for dd, num in enumerate(frame.shape)], frame.dtype
+        ),
+        frame,
+        mat_out * val,
+        axis=3,
+    )
+    main = mid_arr = frame
+    kk = 1
+    while kk < arr_out // 2 + 1:
+        main = ppermute(main, axis_name, [(dd, (dd + 1) % arr_out) for dd in range(arr_out)])
+        now = lax.dynamic_update_slice_in_dim(now, main, (mat_out - kk) % arr_out * val, axis=3)
+        if 2 * kk < arr_out:
+            mid_arr = ppermute(
+                mid_arr, axis_name, [(dd, (dd - 1) % arr_out) for dd in range(arr_out)]
+            )
+            now = lax.dynamic_update_slice_in_dim(
+                now, mid_arr, (mat_out + kk) % arr_out * val, axis=3
+            )
+        kk += 1
+    return now
 
 
 def with_halo(cells, sides, width):
@@ -91,7 +119,7 @@
         for dy in range(3)
         for dx in range(3)
     ]
-    piece = lax.all_gather(w_space, "tm", axis=3, tiled=True)
+    piece = touch_types(w_space)
     total = jnp.zeros((windows[0].shape[0], piece.shape[3]), jnp.float32)
     for dy in range(3):
         for dx in range(3):

time: 246 us -> 272 us (1.11)
  starting transfers between devices: 8.35 us -> 39 us
  waiting for transfers between devices: 37.7 us -> 33.4 us
  matrix products: 13.2 us -> 9.95 us
    all_gather x1 -> x0, waiting for transfers between devices: 36.5 us -> none  [local(): piece = lax.all_gather(w_space, 'tm', axis=3, tiled=True)]
    ppermute x0 -> x15, waiting for transfers between devices: none -> 32.9 us  [the longest x8 32.9 us: touch_types(): ppermute(main, axis_name, [(dd, (dd + 1) % arr_out) for dd in range(arr_o...]
    ppermute x0 -> x15, starting transfers between devices: none -> 32.6 us  [the longest x7 32.1 us: touch_types(): ppermute(mid_arr, axis_name, [(dd, (dd - 1) % arr_out) for dd in range(ar...]
    dot_general x9, matrix products: 7.94 us -> 4.71 us  [local(): jnp.dot(windows[dy * 3 + dx], piece[dy, dx], preferred_element_type=jnp.f...]
  transfers between devices with their start and end apart: 5 -> 19, of which waited for: 2 -> 8; matrix products, arithmetic and copies ran while one was open for 5% -> 4% of each run, Pallas kernels for 0% -> 0%
where the time goes in v1:
time: 272 us; the launch traced here: 270 us
  blocking collectives  61.6 us (23%)
  other arithmetic  43.4 us (16%)
  starting transfers between devices  39 us (14%)
  waiting for transfers between devices  33.4 us (12%)
  between operations  32.5 us (12%)
  loops' own time  31 us (11%)
  local copies, waits for them, and re-layouts  18.7 us (7%)
  matrix products  9.95 us (4%)
    ppermute x8, waiting for transfers between devices, touch_types(): ppermute(main, axis_name, [(dd, (dd + 1) % arr_out) for dd in range(arr_o...  32.9 us
    ppermute x7, starting transfers between devices, touch_types(): ppermute(mid_arr, axis_name, [(dd, (dd - 1) % arr_out) for dd in range(ar...  32.1 us
    another operation x1, loops' own time, entering(): return lax.fori_loop(0, length, step, start)  31 us
    unnamed x1, blocking collectives  30.1 us
    select_n x16, other arithmetic, step(): return jax.tree.map(lambda a, b: jnp.where(reached, a, b), new, before)  25.4 us
    all_to_all x1, blocking collectives, local(): lax.all_to_all(grouped, 'rows', split_axis=0, concat_axis=2, tiled=True)  22.5 us
    gt x16, other arithmetic, join_clip(): pick = late_flag > 0  10.5 us
    dynamic_slice x16, local copies, waits for them, and re-layouts, step(): part[k].astype(own.dtype)  9.82 us
  transfers between devices with their start and end apart: 19, of which 8 were waited for; matrix products, arithmetic and copies ran while one was open for 4% of the time, Pallas kernels for 0%

profile of v1, /device:TPU:0, one launch (start us, length us, event | category | flops | bytes accessed | tf_op | source)
XLA Modules:
  0.0 269.6 jit_solution(15903288565561301001)
XLA Ops:
  7.0 5.1 %collective-permute-start.3 = (bf16[3,3,512,32]{2,3,1,0:T(8,128)(2,1)}, bf16[3,3,512,32]{2,3,1,0:T(8,128)(2,1)S(1)}, u32[]{:S(2)}, u32[]{:S(2)}) collective-permute-start(bf16[3,3,512,32]{2,3,1,0:T(8,128)(2,1)} %param.13), channel_id=1, source_target_pairs={{0,30},{2,0},{4,2},{6,4},{8,6},{10,8},{12,10},{14,12},{16,14},{18,... | collective-permute-start | bytes 884744 | tf_op jit(solution)/shard_map/ppermute | solution.py:25
  15.4 3.8 %collective-permute-start = (bf16[8,1,32,512]{3,2,1,0:T(8,128)(2,1)}, bf16[8,1,32,512]{3,2,1,0:T(8,128)(2,1)S(1)}, u32[]{:S(2)}, u32[]{:S(2)}) collective-permute-start(bf16[8,1,32,512]{3,2,1,0:T(8,128)(2,1)} %get-tuple-element.195), channel_id=1, source_target_pairs={{0,1},{2,3},{4,5},{6,7},{8,9},{10,11},{12,13},{14,15},{16,17},{18,... | collective-permute-start | bytes 786440 | tf_op jit(solution)/shard_map/ppermute | solution.py:43
  31.1 4.4 %collective-permute-start.5 = (bf16[3,3,512,32]{2,3,1,0:T(8,128)(2,1)S(1)}, bf16[3,3,512,32]{2,3,1,0:T(8,128)(2,1)S(1)}, u32[]{:S(2)}, u32[]{:S(2)}) collective-permute-start(bf16[3,3,512,32]{2,3,1,0:T(8,128)(2,1)S(1)} %collective-permute-done.3), channel_id=1, source_target_pairs={{0,30},{2,0},{4,2},{6,4},{8,6},{10,8},{12,10},{14,12},{16,14},{18,... | collective-permute-start | bytes 884744 | tf_op jit(solution)/shard_map/ppermute | solution.py:25
  36.7 3.3 %collective-permute-done.4 = bf16[3,3,512,32]{2,3,1,0:T(8,128)(2,1)S(1)} collective-permute-done((bf16[3,3,512,32]{2,3,1,0:T(8,128)(2,1)S(1)}, bf16[3,3,512,32]{2,3,1,0:T(8,128)(2,1)S(1)}, u32[]{:S(2)}, u32[]{:S(2)}) %collective-permute-start.4) | collective-permute-done | bytes 294944 | tf_op jit(solution)/shard_map/ppermute | solution.py:22
  40.0 4.5 %collective-permute-start.7 = (bf16[3,3,512,32]{2,3,1,0:T(8,128)(2,1)S(1)}, bf16[3,3,512,32]{2,3,1,0:T(8,128)(2,1)S(1)}, u32[]{:S(2)}, u32[]{:S(2)}) collective-permute-start(bf16[3,3,512,32]{2,3,1,0:T(8,128)(2,1)S(1)} %collective-permute-done.5), channel_id=1, source_target_pairs={{0,30},{2,0},{4,2},{6,4},{8,6},{10,8},{12,10},{14,12},{16,14},{18,... | collective-permute-start | bytes 884744 | tf_op jit(solution)/shard_map/ppermute | solution.py:25
  45.1 3.8 %collective-permute-done.6 = bf16[3,3,512,32]{2,3,1,0:T(8,128)(2,1)S(1)} collective-permute-done((bf16[3,3,512,32]{2,3,1,0:T(8,128)(2,1)S(1)}, bf16[3,3,512,32]{2,3,1,0:T(8,128)(2,1)S(1)}, u32[]{:S(2)}, u32[]{:S(2)}) %collective-permute-start.6) | collective-permute-done | bytes 294944 | tf_op jit(solution)/shard_map/ppermute | solution.py:22
  49.1 4.5 %collective-permute-start.9 = (bf16[3,3,512,32]{2,3,1,0:T(8,128)(2,1)S(1)}, bf16[3,3,512,32]{2,3,1,0:T(8,128)(2,1)S(1)}, u32[]{:S(2)}, u32[]{:S(2)}) collective-permute-start(bf16[3,3,512,32]{2,3,1,0:T(8,128)(2,1)S(1)} %collective-permute-done.7), channel_id=1, source_target_pairs={{0,30},{2,0},{4,2},{6,4},{8,6},{10,8},{12,10},{14,12},{16,14},{18,... | collective-permute-start | bytes 884744 | tf_op jit(solution)/shard_map/ppermute | solution.py:25
  53.6 4.3 %collective-permute-done.8 = bf16[3,3,512,32]{2,3,1,0:T(8,128)(2,1)S(1)} collective-permute-done((bf16[3,3,512,32]{2,3,1,0:T(8,128)(2,1)S(1)}, bf16[3,3,512,32]{2,3,1,0:T(8,128)(2,1)S(1)}, u32[]{:S(2)}, u32[]{:S(2)}) %collective-permute-start.8) | collective-permute-done | bytes 294944 | tf_op jit(solution)/shard_map/ppermute | solution.py:22
  58.0 4.6 %collective-permute-start.11 = (bf16[3,3,512,32]{2,3,1,0:T(8,128)(2,1)S(1)}, bf16[3,3,512,32]{2,3,1,0:T(8,128)(2,1)S(1)}, u32[]{:S(2)}, u32[]{:S(2)}) collective-permute-start(bf16[3,3,512,32]{2,3,1,0:T(8,128)(2,1)S(1)} %collective-permute-done.9), channel_id=1, source_target_pairs={{0,30},{2,0},{4,2},{6,4},{8,6},{10,8},{12,10},{14,12},{16,14},{18,... | collective-permute-start | bytes 884744 | tf_op jit(solution)/shard_map/ppermute | solution.py:25
  62.6 4.3 %collective-permute-done.10 = bf16[3,3,512,32]{2,3,1,0:T(8,128)(2,1)S(1)} collective-permute-done((bf16[3,3,512,32]{2,3,1,0:T(8,128)(2,1)S(1)}, bf16[3,3,512,32]{2,3,1,0:T(8,128)(2,1)S(1)}, u32[]{:S(2)}, u32[]{:S(2)}) %collective-permute-start.10) | collective-permute-done | bytes 294944 | tf_op jit(solution)/shard_map/ppermute | solution.py:22
  66.9 4.6 %collective-permute-start.13 = (bf16[3,3,512,32]{2,3,1,0:T(8,128)(2,1)S(1)}, bf16[3,3,512,32]{2,3,1,0:T(8,128)(2,1)S(1)}, u32[]{:S(2)}, u32[]{:S(2)}) collective-permute-start(bf16[3,3,512,32]{2,3,1,0:T(8,128)(2,1)S(1)} %collective-permute-done.11), channel_id=1, source_target_pairs={{0,30},{2,0},{4,2},{6,4},{8,6},{10,8},{12,10},{14,12},{16,14},{18,... | collective-permute-start | bytes 884744 | tf_op jit(solution)/shard_map/ppermute | solution.py:25
  71.5 4.3 %collective-permute-done.12 = bf16[3,3,512,32]{2,3,1,0:T(8,128)(2,1)S(1)} collective-permute-done((bf16[3,3,512,32]{2,3,1,0:T(8,128)(2,1)S(1)}, bf16[3,3,512,32]{2,3,1,0:T(8,128)(2,1)S(1)}, u32[]{:S(2)}, u32[]{:S(2)}) %collective-permute-start.12) | collective-permute-done | bytes 294944 | tf_op jit(solution)/shard_map/ppermute | solution.py:22
  75.9 4.6 %collective-permute-start.15 = (bf16[3,3,512,32]{2,3,1,0:T(8,128)(2,1)S(1)}, bf16[3,3,512,32]{2,3,1,0:T(8,128)(2,1)S(1)}, u32[]{:S(2)}, u32[]{:S(2)}) collective-permute-start(bf16[3,3,512,32]{2,3,1,0:T(8,128)(2,1)S(1)} %collective-permute-done.13), channel_id=1, source_target_pairs={{0,30},{2,0},{4,2},{6,4},{8,6},{10,8},{12,10},{14,12},{16,14},{18,... | collective-permute-start | bytes 884744 | tf_op jit(solution)/shard_map/ppermute | solution.py:25
  80.5 4.2 %collective-permute-done.14 = bf16[3,3,512,32]{2,3,1,0:T(8,128)(2,1)S(1)} collective-permute-done((bf16[3,3,512,32]{2,3,1,0:T(8,128)(2,1)S(1)}, bf16[3,3,512,32]{2,3,1,0:T(8,128)(2,1)S(1)}, u32[]{:S(2)}, u32[]{:S(2)}) %collective-permute-start.14) | collective-permute-done | bytes 294944 | tf_op jit(solution)/shard_map/ppermute | solution.py:22
  84.8 8.7 %collective-permute-done.16 = bf16[3,3,512,32]{2,3,1,0:T(8,128)(2,1)S(1)} collective-permute-done((bf16[3,3,512,32]{2,3,1,0:T(8,128)(2,1)S(1)}, bf16[3,3,512,32]{2,3,1,0:T(8,128)(2,1)S(1)}, u32[]{:S(2)}, u32[]{:S(2)}) %collective-permute-start.16) | collective-permute-done | bytes 294944 | tf_op jit(solution)/shard_map/ppermute | solution.py:22
  105.9 30.1 %all-reduce.4 = (bf16[16]{0:T(256)(128)(2,1)S(1)}, bf16[16]{0:T(256)(128)(2,1)S(1)}) all-reduce(bf16[16]{0:T(256)(128)(2,1)S(1)} %dynamic-update-slice, bf16[16]{0:T(256)(128)(2,1)S(1)} %dynamic-update-slice.1), channel_id=2, replica_groups=mesh['tm'=16,'rows'=2] {'tm'}, use_global_device_ids=true, to_apply=%add.2 | all-reduce | flops 32 | bytes 128
  146.2 76.8 %while.16 = (s32[]{:T(128)}, f32[2,32,512]{2,1,0:T(8,128)S(1)}, f32[1]{0:T(128)}, s32[]{:T(128)}, bf16[16,1]{0,1:T(2,128)(2,1)S(1)}, /*index=5*/bf16[16,2,32,512...) while((s32[]{:T(128)}, f32[2,32,512]{2,1,0:T(8,128)S(1)}, f32[1]{0:T(128)}, ...), condition=%wide.region_2.3_spmd.clone, body=%wide.region_1.2_spmd.clone.sunk | while | flops 163849 | bytes 327847 | solution.py:78
  149.4 1.6 fusion.73
  154.2 1.6 fusion.73
  159.0 1.6 fusion.73
  163.8 1.6 fusion.73
  168.6 1.6 fusion.73
  173.4 1.6 fusion.73
  178.2 1.6 fusion.73
  183.0 1.6 fusion.73
  187.8 1.6 fusion.73
  192.6 1.6 fusion.73
  197.4 1.6 fusion.73
  202.2 1.6 fusion.73
  207.0 1.6 fusion.73
  226.8 22.5 %all_to_all.30 = bf16[2,4,2,32,1536]{4,3,2,1,0:T(8,128)(2,1)S(1)} all-to-all(bf16[2,4,2,32,1536]{4,3,2,1,0:T(8,128)(2,1)S(1)} %bitcast.175), channel_id=1, replica_groups=mesh['tm'=16,'rows'=2] {'rows'}, dimensions={0} | all-to-all | bytes 3145728 | tf_op jit(solution)/shard_map/all_to_all | solution.py:176
  252.4 9.1 %all_to_all.31 = bf16[1,4,4,32,512]{4,3,1,0,2:T(8,128)(2,1)S(1)} all-to-all(bf16[1,4,4,32,512]{4,3,1,0,2:T(8,128)(2,1)S(1)} %copy.18), channel_id=1, replica_groups=mesh['tm'=16,'rows'=2] {'rows'}, dimensions={2} | all-to-all | bytes 1048576 | tf_op jit(solution)/shard_map/all_to_all | solution.py:181
  (146 shorter events, 55.0 us)
Async XLA Ops:
  6.5 219.2 %copy-start = (bf16[512,1536]{1,0:T(8,128)(2,1)S(1)}, bf16[512,1536]{1,0:T(8,128)(2,1)}, u32[]{:S(2)}) copy-start(bf16[512,1536]{1,0:T(8,128)(2,1)} %param.16) | copy-start | bytes 4718596
  6.5 29.4 %copy-start.5 = (bf16[3,3,512,32]{2,3,1,0:T(8,128)(2,1)S(1)}, bf16[3,3,512,32]{2,3,1,0:T(8,128)(2,1)}, u32[]{:S(2)}) copy-start(bf16[3,3,512,32]{2,3,1,0:T(8,128)(2,1)} %param.13) | copy-start | bytes 884740
  6.5 139.6 %all-gather.3.cloned.1.call-start = ((), (), s32[]{:S(2)}) async-start(), calls=%async_computation.2 | async-start | bytes 1114112 | tf_op jit(solution)/shard_map/all_gather | solution.py:61
  6.5 24.5 %collective-permute-start.2 = (bf16[3,3,512,32]{2,3,1,0:T(8,128)(2,1)}, bf16[3,3,512,32]{2,3,1,0:T(8,128)(2,1)S(1)}, u32[]{:S(2)}, u32[]{:S(2)}) collective-permute-start(bf16[3,3,512,32]{2,3,1,0:T(8,128)(2,1)} %param.13), channel_id=1, source_target_pairs={{0,2},{2,4},{4,6},{6,8},{8,10},{10,12},{12,14},{14,16},{16,18},{18... | collective-permute-start | bytes 884744 | tf_op jit(solution)/shard_map/ppermute | solution.py:22
  7.0 24.1 %collective-permute-start.3 = (bf16[3,3,512,32]{2,3,1,0:T(8,128)(2,1)}, bf16[3,3,512,32]{2,3,1,0:T(8,128)(2,1)S(1)}, u32[]{:S(2)}, u32[]{:S(2)}) collective-permute-start(bf16[3,3,512,32]{2,3,1,0:T(8,128)(2,1)} %param.13), channel_id=1, source_target_pairs={{0,30},{2,0},{4,2},{6,4},{8,6},{10,8},{12,10},{14,12},{16,14},{18,... | collective-permute-start | bytes 884744 | tf_op jit(solution)/shard_map/ppermute | solution.py:25
  15.4 20.6 %collective-permute-start = (bf16[8,1,32,512]{3,2,1,0:T(8,128)(2,1)}, bf16[8,1,32,512]{3,2,1,0:T(8,128)(2,1)S(1)}, u32[]{:S(2)}, u32[]{:S(2)}) collective-permute-start(bf16[8,1,32,512]{3,2,1,0:T(8,128)(2,1)} %get-tuple-element.195), channel_id=1, source_target_pairs={{0,1},{2,3},{4,5},{6,7},{8,9},{10,11},{12,13},{14,15},{16,17},{18,... | collective-permute-start | bytes 786440 | tf_op jit(solution)/shard_map/ppermute | solution.py:43
  19.2 16.8 %collective-permute-start.1 = (bf16[8,1,32,512]{3,2,1,0:T(8,128)(2,1)}, bf16[8,1,32,512]{3,2,1,0:T(8,128)(2,1)S(1)}, u32[]{:S(2)}, u32[]{:S(2)}) collective-permute-start(bf16[8,1,32,512]{3,2,1,0:T(8,128)(2,1)} %get-tuple-element.196), channel_id=1, source_target_pairs={{1,0},{3,2},{5,4},{7,6},{9,8},{11,10},{13,12},{15,14},{17,16},{19,... | collective-permute-start | bytes 786440 | tf_op jit(solution)/shard_map/ppermute | solution.py:45
  31.1 8.9 %collective-permute-start.4 = (bf16[3,3,512,32]{2,3,1,0:T(8,128)(2,1)S(1)}, bf16[3,3,512,32]{2,3,1,0:T(8,128)(2,1)S(1)}, u32[]{:S(2)}, u32[]{:S(2)}) collective-permute-start(bf16[3,3,512,32]{2,3,1,0:T(8,128)(2,1)S(1)} %collective-permute-done.2), channel_id=1, source_target_pairs={{0,2},{2,4},{4,6},{6,8},{8,10},{10,12},{12,14},{14,16},{16,18},{18... | collective-permute-start | bytes 884744 | tf_op jit(solution)/shard_map/ppermute | solution.py:22
  31.1 8.9 %collective-permute-start.5 = (bf16[3,3,512,32]{2,3,1,0:T(8,128)(2,1)S(1)}, bf16[3,3,512,32]{2,3,1,0:T(8,128)(2,1)S(1)}, u32[]{:S(2)}, u32[]{:S(2)}) collective-permute-start(bf16[3,3,512,32]{2,3,1,0:T(8,128)(2,1)S(1)} %collective-permute-done.3), channel_id=1, source_target_pairs={{0,30},{2,0},{4,2},{6,4},{8,6},{10,8},{12,10},{14,12},{16,14},{18,... | collective-permute-start | bytes 884744 | tf_op jit(solution)/shard_map/ppermute | solution.py:25
  40.0 8.9 %collective-permute-start.6 = (bf16[3,3,512,32]{2,3,1,0:T(8,128)(2,1)S(1)}, bf16[3,3,512,32]{2,3,1,0:T(8,128)(2,1)S(1)}, u32[]{:S(2)}, u32[]{:S(2)}) collective-permute-start(bf16[3,3,512,32]{2,3,1,0:T(8,128)(2,1)S(1)} %collective-permute-done.4), channel_id=1, source_target_pairs={{0,2},{2,4},{4,6},{6,8},{8,10},{10,12},{12,14},{14,16},{16,18},{18... | collective-permute-start | bytes 884744 | tf_op jit(solution)/shard_map/ppermute | solution.py:22
  40.0 9.1 %collective-permute-start.7 = (bf16[3,3,512,32]{2,3,1,0:T(8,128)(2,1)S(1)}, bf16[3,3,512,32]{2,3,1,0:T(8,128)(2,1)S(1)}, u32[]{:S(2)}, u32[]{:S(2)}) collective-permute-start(bf16[3,3,512,32]{2,3,1,0:T(8,128)(2,1)S(1)} %collective-permute-done.5), channel_id=1, source_target_pairs={{0,30},{2,0},{4,2},{6,4},{8,6},{10,8},{12,10},{14,12},{16,14},{18,... | collective-permute-start | bytes 884744 | tf_op jit(solution)/shard_map/ppermute | solution.py:25
  48.9 8.9 %collective-permute-start.8 = (bf16[3,3,512,32]{2,3,1,0:T(8,128)(2,1)S(1)}, bf16[3,3,512,32]{2,3,1,0:T(8,128)(2,1)S(1)}, u32[]{:S(2)}, u32[]{:S(2)}) collective-permute-start(bf16[3,3,512,32]{2,3,1,0:T(8,128)(2,1)S(1)} %collective-permute-done.6), channel_id=1, source_target_pairs={{0,2},{2,4},{4,6},{6,8},{8,10},{10,12},{12,14},{14,16},{16,18},{18... | collective-permute-start | bytes 884744 | tf_op jit(solution)/shard_map/ppermute | solution.py:22
  49.1 8.9 %collective-permute-start.9 = (bf16[3,3,512,32]{2,3,1,0:T(8,128)(2,1)S(1)}, bf16[3,3,512,32]{2,3,1,0:T(8,128)(2,1)S(1)}, u32[]{:S(2)}, u32[]{:S(2)}) collective-permute-start(bf16[3,3,512,32]{2,3,1,0:T(8,128)(2,1)S(1)} %collective-permute-done.7), channel_id=1, source_target_pairs={{0,30},{2,0},{4,2},{6,4},{8,6},{10,8},{12,10},{14,12},{16,14},{18,... | collective-permute-start | bytes 884744 | tf_op jit(solution)/shard_map/ppermute | solution.py:25
  57.9 8.9 %collective-permute-start.10 = (bf16[3,3,512,32]{2,3,1,0:T(8,128)(2,1)S(1)}, bf16[3,3,512,32]{2,3,1,0:T(8,128)(2,1)S(1)}, u32[]{:S(2)}, u32[]{:S(2)}) collective-permute-start(bf16[3,3,512,32]{2,3,1,0:T(8,128)(2,1)S(1)} %collective-permute-done.8), channel_id=1, source_target_pairs={{0,2},{2,4},{4,6},{6,8},{8,10},{10,12},{12,14},{14,16},{16,18},{18... | collective-permute-start | bytes 884744 | tf_op jit(solution)/shard_map/ppermute | solution.py:22
  58.0 8.9 %collective-permute-start.11 = (bf16[3,3,512,32]{2,3,1,0:T(8,128)(2,1)S(1)}, bf16[3,3,512,32]{2,3,1,0:T(8,128)(2,1)S(1)}, u32[]{:S(2)}, u32[]{:S(2)}) collective-permute-start(bf16[3,3,512,32]{2,3,1,0:T(8,128)(2,1)S(1)} %collective-permute-done.9), channel_id=1, source_target_pairs={{0,30},{2,0},{4,2},{6,4},{8,6},{10,8},{12,10},{14,12},{16,14},{18,... | collective-permute-start | bytes 884744 | tf_op jit(solution)/shard_map/ppermute | solution.py:25
  66.8 8.9 %collective-permute-start.12 = (bf16[3,3,512,32]{2,3,1,0:T(8,128)(2,1)S(1)}, bf16[3,3,512,32]{2,3,1,0:T(8,128)(2,1)S(1)}, u32[]{:S(2)}, u32[]{:S(2)}) collective-permute-start(bf16[3,3,512,32]{2,3,1,0:T(8,128)(2,1)S(1)} %collective-permute-done.10), channel_id=1, source_target_pairs={{0,2},{2,4},{4,6},{6,8},{8,10},{10,12},{12,14},{14,16},{16,18},{18... | collective-permute-start | bytes 884744 | tf_op jit(solution)/shard_map/ppermute | solution.py:22
  66.9 8.9 %collective-permute-start.13 = (bf16[3,3,512,32]{2,3,1,0:T(8,128)(2,1)S(1)}, bf16[3,3,512,32]{2,3,1,0:T(8,128)(2,1)S(1)}, u32[]{:S(2)}, u32[]{:S(2)}) collective-permute-start(bf16[3,3,512,32]{2,3,1,0:T(8,128)(2,1)S(1)} %collective-permute-done.11), channel_id=1, source_target_pairs={{0,30},{2,0},{4,2},{6,4},{8,6},{10,8},{12,10},{14,12},{16,14},{18,... | collective-permute-start | bytes 884744 | tf_op jit(solution)/shard_map/ppermute | solution.py:25
  75.8 8.8 %collective-permute-start.14 = (bf16[3,3,512,32]{2,3,1,0:T(8,128)(2,1)S(1)}, bf16[3,3,512,32]{2,3,1,0:T(8,128)(2,1)S(1)}, u32[]{:S(2)}, u32[]{:S(2)}) collective-permute-start(bf16[3,3,512,32]{2,3,1,0:T(8,128)(2,1)S(1)} %collective-permute-done.12), channel_id=1, source_target_pairs={{0,2},{2,4},{4,6},{6,8},{8,10},{10,12},{12,14},{14,16},{16,18},{18... | collective-permute-start | bytes 884744 | tf_op jit(solution)/shard_map/ppermute | solution.py:22
  75.9 8.8 %collective-permute-start.15 = (bf16[3,3,512,32]{2,3,1,0:T(8,128)(2,1)S(1)}, bf16[3,3,512,32]{2,3,1,0:T(8,128)(2,1)S(1)}, u32[]{:S(2)}, u32[]{:S(2)}) collective-permute-start(bf16[3,3,512,32]{2,3,1,0:T(8,128)(2,1)S(1)} %collective-permute-done.13), channel_id=1, source_target_pairs={{0,30},{2,0},{4,2},{6,4},{8,6},{10,8},{12,10},{14,12},{16,14},{18,... | collective-permute-start | bytes 884744 | tf_op jit(solution)/shard_map/ppermute | solution.py:25
  84.6 8.8 %collective-permute-start.16 = (bf16[3,3,512,32]{2,3,1,0:T(8,128)(2,1)S(1)}, bf16[3,3,512,32]{2,3,1,0:T(8,128)(2,1)S(1)}, u32[]{:S(2)}, u32[]{:S(2)}) collective-permute-start(bf16[3,3,512,32]{2,3,1,0:T(8,128)(2,1)S(1)} %collective-permute-done.14), channel_id=1, source_target_pairs={{0,2},{2,4},{4,6},{6,8},{8,10},{10,12},{12,14},{14,16},{16,18},{18... | collective-permute-start | bytes 884744 | tf_op jit(solution)/shard_map/ppermute | solution.py:22
  97.3 2.3 copy-start.1
  97.3 2.3 copy-start.3
  98.3 2.3 collective-permute-start.17
  100.6 2.4 copy-start.7
  101.6 124.0 %copy-start.6 = (f32[512]{0:T(512)S(1)}, f32[512]{0:T(512)}, u32[]{:S(2)}) copy-start(f32[512]{0:T(512)} %param.15) | copy-start | bytes 6148
  249.2 12.3 %copy-start.4 = (bf16[512,512]{1,0:T(8,128)(2,1)S(1)}, bf16[512,512]{1,0:T(8,128)(2,1)}, u32[]{:S(2)}) copy-start(bf16[512,512]{1,0:T(8,128)(2,1)} %param.17) | copy-start | bytes 1572868
  249.4 1.2 copy-start.2
Sparse Core Ops, SparseCore 0:
  102.5 39.4 all-gather.2
